TPU v7x, 128 devices: a whole 4x4x4 slice. The times are simulated.
128 devices in a mesh: probe: 4 (over z_hi, core), sx: 4 (over x), sy: 8 (over y, z_lo).
Axes of the slice: x: 4, y: 4, z: 4 (z_hi: 2, z_lo: 2; z = z_hi * 2 + z_lo), core: 2. Of those that a mesh axis runs over, the one named last changes fastest.
Arguments:
- probes: float32 [8, 128, 256, 256], P('probe', 'sx', 'sy'), may hold values from -6 to 6
- velocity: float32 [3, 128, 256, 256], P(None, 'sx', 'sy'), may hold values from -0.15 to 0.15
- diffusivity: float32 [128, 256, 256], P('sx', 'sy'), may hold values from 0.02 to 0.15
- obs_weight: float32 [128, 256, 256], P('sx', 'sy'), may hold values from 0.05 to 1
Outputs:
- basis_fields: float32 [8, 128, 256, 256], P('probe', 'sx', 'sy')
- projected_hessian: float32 [8, 8], replicated
All inputs are finite; a program needn't handle non-finite values.
Results may differ from a plain program's by a relative error of at most 0.00013.
Values sent between devices are 32-bit elements; how exact they have to be, the bound alone decides.
A program may use at most 128 MiB of HBM per device.

v0:
```python
import jax
import jax.numpy as jnp
from jax import lax
from jax.sharding import PartitionSpec as P

STEPS = 4


def extended(value, sides, width):
    for axis, dim in sides:
        devices, length = (lax.axis_size(axis), value.shape[dim])
        up = [(i, (i + 1) % devices) for i in range(devices - 1)]
        down = [(j, i) for i, j in up]
        last = lax.slice_in_dim(value, length - width, length, axis=dim)
        leading = lax.slice_in_dim(value, 0, width, axis=dim)
        before = lax.ppermute(last, axis, up)
        after = lax.ppermute(leading, axis, down)
        value = jnp.concatenate([before, value, after], axis=dim)
    return value


def forward_step(state, coeffs):
    cc = coeffs[:, 1:-1, 1:-1, :]
    spread = cc[0]
    inner = state[:, 1:-1, 1:-1, :]
    padded = jnp.pad(inner, ((0, 0), (0, 0), (0, 0), (1, 1)))
    result = (1.0 - 6.0 * spread) * inner
    result = (
        result
        + (spread - 0.5 * cc[1]) * state[:, 2:, 1:-1, :]
        + (spread + 0.5 * cc[1]) * state[:, :-2, 1:-1, :]
    )
    result = (
        result
        + (spread - 0.5 * cc[2]) * state[:, 1:-1, 2:, :]
        + (spread + 0.5 * cc[2]) * state[:, 1:-1, :-2, :]
    )
    result = (
        result
        + (spread - 0.5 * cc[3]) * padded[..., 2:]
        + (spread + 0.5 * cc[3]) * padded[..., :-2]
    )
    return result


def adjoint_step(state, coeffs):
    spread = coeffs[0]
    plus_x = (spread - 0.5 * coeffs[1]) * state
    minus_x = (spread + 0.5 * coeffs[1]) * state
    plus_y = (spread - 0.5 * coeffs[2]) * state
    minus_y = (spread + 0.5 * coeffs[2]) * state
    cc = coeffs[:, 1:-1, 1:-1, :]
    inner = state[:, 1:-1, 1:-1, :]
    pad_plus = jnp.pad((cc[0] - 0.5 * cc[3]) * inner, ((0, 0), (0, 0), (0, 0), (1, 1)))
    pad_minus = jnp.pad((cc[0] + 0.5 * cc[3]) * inner, ((0, 0), (0, 0), (0, 0), (1, 1)))
    result = (1.0 - 6.0 * cc[0]) * inner
    result = result + plus_x[:, :-2, 1:-1, :] + minus_x[:, 2:, 1:-1, :]
    result = result + plus_y[:, 1:-1, :-2, :] + minus_y[:, 1:-1, 2:, :]
    result = result + pad_plus[..., :-2] + pad_minus[..., 2:]
    return result


def factor_inverse(gram, count):
    lower = jnp.linalg.cholesky(gram)
    return jax.scipy.linalg.solve_triangular(lower, jnp.eye(count, dtype=jnp.float32), lower=True)


def shards(probes, velocity, diffusivity, obs_weight):
    group = probes.shape[0]
    count = group * lax.axis_size("probe")
    ncells = (
        probes.shape[1]
        * probes.shape[2]
        * probes.shape[3]
        * lax.axis_size("sx")
        * lax.axis_size("sy")
    )
    coeffs = jnp.concatenate([diffusivity[None], velocity], axis=0)
    highest = lax.Precision.HIGHEST
    edge_coeffs = extended(coeffs, (("sx", 1), ("sy", 2)), 1)

    def forward(state):
        for step in range(STEPS):
            padded = extended(state, (("sx", 1), ("sy", 2)), 1)
            state = forward_step(padded, edge_coeffs)
        return state

    state = obs_weight * forward(probes)
    for step in range(STEPS):
        padded = extended(state, (("sx", 1), ("sy", 2)), 1)
        state = adjoint_step(padded, edge_coeffs)
    images = state
    again = forward(images)
    root = jnp.sqrt(obs_weight) * again
    both = jnp.stack([images, root], axis=1)
    slabs = lax.all_to_all(both, "probe", split_axis=2, concat_axis=0, tiled=True)
    flat = slabs[:, 0].reshape(count, -1)
    flat_root = slabs[:, 1].reshape(count, -1)
    partial_gram = jnp.dot(flat, flat.T, precision=highest)
    partial_cross = jnp.dot(flat_root, flat_root.T, precision=highest)
    sums = lax.psum(jnp.stack([partial_gram, partial_cross]), ("probe", "sx", "sy")) / ncells
    gram, cross = (sums[0], sums[1])
    inverse = factor_inverse(gram, count)
    basis_slab = jnp.dot(inverse, flat, precision=highest)
    basis_fields = lax.all_to_all(
        basis_slab.reshape(slabs[:, 0].shape), "probe", split_axis=0, concat_axis=1, tiled=True
    )
    projected = jnp.dot(jnp.dot(inverse, cross, precision=highest), inverse.T, precision=highest)
    return (basis_fields, projected)


def solution(mesh):
    return jax.shard_map(
        shards,
        mesh=mesh,
        in_specs=(
            P("probe", "sx", "sy", None),
            P(None, "sx", "sy", None),
            P("sx", "sy", None),
            P("sx", "sy", None),
        ),
        out_specs=(P("probe", "sx", "sy", None), P()),
        check_vma=False,
    )
```

profile of v0, /device:TPU:1, one launch (start us, length us, event | category | flops | bytes accessed | tf_op | source)
XLA Modules:
  0.0 471.6 jit_solution(13638757533432052887)
XLA Ops:
  3.0 4.6 collective-permute-start.1
  12.0 4.4 collective-permute-start.3
  33.3 4.9 %collective-permute-start.7 = (f32[2,34,1,256]{3,1,2,0:T(8,128)S(1)}, f32[2,34,1,256]{3,1,2,0:T(8,128)S(1)}, u32[]{:S(2)}, u32[]{:S(2)}) collective-permute-start(f32[2,34,1,256]{3,1,2,0:T(8,128)S(1)} %get-tuple-element.46), channel_id=1, source_target_pairs={{0,1},{1,2},{2,3},{3,4},{4,5},{5,6},{6,7},{8,9},{9,10},{10,11},{11... | collective-permute-start | bytes 208904 | tf_op jit(solution)/shard_map/ppermute | solution.py:16
  48.4 4.6 collective-permute-start.9
  53.3 4.4 collective-permute-start.18
  60.4 4.8 %collective-permute-start.11 = (f32[2,34,1,256]{3,1,2,0:T(8,128)S(1)}, f32[2,34,1,256]{3,1,2,0:T(8,128)S(1)}, u32[]{:S(2)}, u32[]{:S(2)}) collective-permute-start(f32[2,34,1,256]{3,1,2,0:T(8,128)S(1)} %get-tuple-element.44), channel_id=1, source_target_pairs={{0,1},{1,2},{2,3},{3,4},{4,5},{5,6},{6,7},{8,9},{9,10},{10,11},{11... | collective-permute-start | bytes 208904 | tf_op jit(solution)/shard_map/ppermute | solution.py:16
  73.1 4.3 collective-permute-start.13
  80.0 4.4 collective-permute-start.15
  98.3 4.3 collective-permute-start.22
  122.1 4.3 collective-permute-start.26
  165.1 4.3 collective-permute-start.34
  203.5 4.4 collective-permute-start.43
  215.3 4.4 collective-permute-start.45
  222.4 4.4 collective-permute-start.47
  233.2 4.6 collective-permute-start.49
  240.4 5.3 %collective-permute-start.51 = (f32[2,34,1,256]{3,1,2,0:T(8,128)S(1)}, f32[2,34,1,256]{3,1,2,0:T(8,128)S(1)}, u32[]{:S(2)}, u32[]{:S(2)}) collective-permute-start(f32[2,34,1,256]{3,1,2,0:T(8,128)S(1)} %get-tuple-element.26), channel_id=1, source_target_pairs={{0,1},{1,2},{2,3},{3,4},{4,5},{5,6},{6,7},{8,9},{9,10},{10,11},{11... | collective-permute-start | bytes 208904 | tf_op jit(solution)/shard_map/ppermute | solution.py:16
  253.3 79.6 %all_to_all.36 = f32[2,2,32,32,256]{4,3,0,1,2:T(8,128)S(1)} all-to-all(f32[2,2,32,32,256]{4,3,0,1,2:T(8,128)S(1)} %copy.58), channel_id=1, replica_groups=mesh['probe'=4,'sx'=4,'sy'=8] {'probe'}, dimensions={2} | all-to-all | bytes 8388608 | tf_op jit(solution)/shard_map/all_to_all | solution.py:96
  333.0 5.2 %copy.72 = f32[2,2,4,8,32,256]{5,0,2,4,3,1:T(2,128)} copy(f32[2,2,4,8,32,256]{5,4,0,1,3,2:T(8,128)S(1)} %bitcast.90) | data formatting | bytes 8388608 | tf_op jit(solution)/shard_map/all_to_all | solution.py:96
  338.2 6.1 %all_to_all.29 = f32[8,2,8,32,256]{4,0,3,2,1:T(8,128)} reshape(f32[4,2,2,8,32,256]{5,1,0,4,3,2:T(2,128)} %bitcast.91) | data formatting | bytes 8388608 | tf_op jit(solution)/shard_map/all_to_all | solution.py:96
  344.4 7.1 %fusion.131 = f32[1,8,8]{2,1,0:T(8,128)S(1)} fusion(f32[8,2,8,32,256]{4,0,3,2,1:T(8,128)} %all_to_all.29), kind=kOutput, calls=%fused_computation.253 | convolution fusion | flops 50331648 | bytes 2097408 | tf_op jit(solution)/shard_map/dot_general | solution.py:99
  351.5 7.1 %fusion.134 = f32[1,8,8]{2,1,0:T(8,128)S(1)} fusion(f32[8,2,8,32,256]{4,0,3,2,1:T(8,128)} %all_to_all.29), kind=kOutput, calls=%fused_computation.254 | convolution fusion | flops 50331648 | bytes 2097408 | tf_op jit(solution)/shard_map/dot_general | solution.py:100
  358.6 72.6 %psum.7 = f32[2,8,8]{2,1,0:T(8,128)S(1)} all-reduce(f32[2,8,8]{2,1,0:T(8,128)S(1)} %pad_maximum_fusion.117), channel_id=1, replica_groups=mesh['probe'=4,'sx'=4,'sy'=8] {'probe','sx','sy'}, use_global_device_ids=true, to_apply=%region_0.1 | all-reduce | flops 128 | bytes 1024 | tf_op jit(solution)/shard_map/psum | solution.py:101
  439.6 4.1 all-to-all-start.1
  444.6 25.3 %all-to-all-done.1 = f32[8,8,32,256]{3,2,1,0:T(8,128)S(1)} async-done(((f32[8,8,32,256]{3,2,1,0:T(8,128)}), f32[8,8,32,256]{3,2,1,0:T(8,128)S(1)}, u32[]{:S(2)}, u32[]{:S(2)}) %all-to-all-start.1) | async-done | bytes 2097184 | tf_op jit(solution)/shard_map/all_to_all | solution.py:105
  (191 shorter events, 189.7 us)
Async XLA Ops:
  1.6 8.9 %collective-permute-start = (f32[2,1,32,256]{3,1,2,0:T(1,128)S(1)}, f32[2,1,32,256]{3,1,2,0:T(1,128)S(1)}, u32[]{:S(2)}, u32[]{:S(2)}) collective-permute-start(f32[2,1,32,256]{3,1,2,0:T(1,128)S(1)} %copy.38), channel_id=1, source_target_pairs={{8,0},{16,8},{24,16},{9,1},{17,9},{25,17},{10,2},{18,10},{26,18},{... | collective-permute-start | bytes 196616 | tf_op jit(solution)/shard_map/ppermute | solution.py:17
  3.0 7.6 %collective-permute-start.1 = (f32[2,1,32,256]{3,1,2,0:T(1,128)S(1)}, f32[2,1,32,256]{3,1,2,0:T(1,128)S(1)}, u32[]{:S(2)}, u32[]{:S(2)}) collective-permute-start(f32[2,1,32,256]{3,1,2,0:T(1,128)S(1)} %copy.41), channel_id=1, source_target_pairs={{0,8},{8,16},{16,24},{1,9},{9,17},{17,25},{2,10},{10,18},{18,26},{... | collective-permute-start | bytes 196616 | tf_op jit(solution)/shard_map/ppermute | solution.py:16
  10.6 11.2 %collective-permute-start.2 = (f32[2,34,1,256]{3,1,2,0:T(8,128)S(1)}, f32[2,34,1,256]{3,1,2,0:T(8,128)S(1)}, u32[]{:S(2)}, u32[]{:S(2)}) collective-permute-start(f32[2,34,1,256]{3,1,2,0:T(8,128)S(1)} %get-tuple-element.47), channel_id=1, source_target_pairs={{1,0},{2,1},{3,2},{4,3},{5,4},{6,5},{7,6},{9,8},{10,9},{11,10},{12... | collective-permute-start | bytes 208904 | tf_op jit(solution)/shard_map/ppermute | solution.py:17
  12.0 9.8 %collective-permute-start.3 = (f32[2,34,1,256]{3,1,2,0:T(8,128)S(1)}, f32[2,34,1,256]{3,1,2,0:T(8,128)S(1)}, u32[]{:S(2)}, u32[]{:S(2)}) collective-permute-start(f32[2,34,1,256]{3,1,2,0:T(8,128)S(1)} %get-tuple-element.48), channel_id=1, source_target_pairs={{0,1},{1,2},{2,3},{3,4},{4,5},{5,6},{6,7},{8,9},{9,10},{10,11},{11... | collective-permute-start | bytes 208904 | tf_op jit(solution)/shard_map/ppermute | solution.py:16
  32.0 11.5 %collective-permute-start.6 = (f32[2,34,1,256]{3,1,2,0:T(8,128)S(1)}, f32[2,34,1,256]{3,1,2,0:T(8,128)S(1)}, u32[]{:S(2)}, u32[]{:S(2)}) collective-permute-start(f32[2,34,1,256]{3,1,2,0:T(8,128)S(1)} %get-tuple-element.45), channel_id=1, source_target_pairs={{1,0},{2,1},{3,2},{4,3},{5,4},{6,5},{7,6},{9,8},{10,9},{11,10},{12... | collective-permute-start | bytes 208904 | tf_op jit(solution)/shard_map/ppermute | solution.py:17
  33.3 10.2 %collective-permute-start.7 = (f32[2,34,1,256]{3,1,2,0:T(8,128)S(1)}, f32[2,34,1,256]{3,1,2,0:T(8,128)S(1)}, u32[]{:S(2)}, u32[]{:S(2)}) collective-permute-start(f32[2,34,1,256]{3,1,2,0:T(8,128)S(1)} %get-tuple-element.46), channel_id=1, source_target_pairs={{0,1},{1,2},{2,3},{3,4},{4,5},{5,6},{6,7},{8,9},{9,10},{10,11},{11... | collective-permute-start | bytes 208904 | tf_op jit(solution)/shard_map/ppermute | solution.py:16
  38.3 14.8 %collective-permute-start.16 = (f32[4,1,32,256]{3,2,1,0:T(8,128)S(1)}, f32[4,1,32,256]{3,2,1,0:T(8,128)S(1)}, u32[]{:S(2)}, u32[]{:S(2)}) collective-permute-start(f32[4,1,32,256]{3,2,1,0:T(8,128)S(1)} %get-tuple-element.17), channel_id=1, source_target_pairs={{0,8},{8,16},{16,24},{1,9},{9,17},{17,25},{2,10},{10,18},{18,26},{... | collective-permute-start | bytes 393224 | tf_op jit(solution)/shard_map/ppermute | solution.py:16
  42.3 10.8 %collective-permute-start.17 = (f32[4,1,32,256]{3,2,1,0:T(8,128)S(1)}, f32[4,1,32,256]{3,2,1,0:T(8,128)S(1)}, u32[]{:S(2)}, u32[]{:S(2)}) collective-permute-start(f32[4,1,32,256]{3,2,1,0:T(8,128)S(1)} %get-tuple-element.18), channel_id=1, source_target_pairs={{8,0},{16,8},{24,16},{9,1},{17,9},{25,17},{10,2},{18,10},{26,18},{... | collective-permute-start | bytes 393224 | tf_op jit(solution)/shard_map/ppermute | solution.py:17
  47.1 11.9 %collective-permute-start.8 = (f32[2,1,32,256]{3,1,2,0:T(1,128)S(1)}, f32[2,1,32,256]{3,1,2,0:T(1,128)S(1)}, u32[]{:S(2)}, u32[]{:S(2)}) collective-permute-start(f32[2,1,32,256]{3,1,2,0:T(1,128)S(1)} %get-tuple-element.68), channel_id=1, source_target_pairs={{8,0},{16,8},{24,16},{9,1},{17,9},{25,17},{10,2},{18,10},{26,18},{... | collective-permute-start | bytes 196616 | tf_op jit(solution)/shard_map/ppermute | solution.py:17
  48.4 10.6 %collective-permute-start.9 = (f32[2,1,32,256]{3,1,2,0:T(1,128)S(1)}, f32[2,1,32,256]{3,1,2,0:T(1,128)S(1)}, u32[]{:S(2)}, u32[]{:S(2)}) collective-permute-start(f32[2,1,32,256]{3,1,2,0:T(1,128)S(1)} %get-tuple-element.67), channel_id=1, source_target_pairs={{0,8},{8,16},{16,24},{1,9},{9,17},{17,25},{2,10},{10,18},{18,26},{... | collective-permute-start | bytes 196616 | tf_op jit(solution)/shard_map/ppermute | solution.py:16
  53.3 12.5 %collective-permute-start.18 = (f32[4,34,1,256]{3,1,2,0:T(8,128)S(1)}, f32[4,34,1,256]{3,1,2,0:T(8,128)S(1)}, u32[]{:S(2)}, u32[]{:S(2)}) collective-permute-start(f32[4,34,1,256]{3,1,2,0:T(8,128)S(1)} %copy.49), channel_id=1, source_target_pairs={{0,1},{1,2},{2,3},{3,4},{4,5},{5,6},{6,7},{8,9},{9,10},{10,11},{11... | collective-permute-start | bytes 417800 | tf_op jit(solution)/shard_map/ppermute | solution.py:16
  57.8 8.2 %collective-permute-start.19 = (f32[4,34,1,256]{3,1,2,0:T(8,128)S(1)}, f32[4,34,1,256]{3,1,2,0:T(8,128)S(1)}, u32[]{:S(2)}, u32[]{:S(2)}) collective-permute-start(f32[4,34,1,256]{3,1,2,0:T(8,128)S(1)} %copy.50), channel_id=1, source_target_pairs={{1,0},{2,1},{3,2},{4,3},{5,4},{6,5},{7,6},{9,8},{10,9},{11,10},{12... | collective-permute-start | bytes 417800 | tf_op jit(solution)/shard_map/ppermute | solution.py:17
  59.1 7.1 %collective-permute-start.10 = (f32[2,34,1,256]{3,1,2,0:T(8,128)S(1)}, f32[2,34,1,256]{3,1,2,0:T(8,128)S(1)}, u32[]{:S(2)}, u32[]{:S(2)}) collective-permute-start(f32[2,34,1,256]{3,1,2,0:T(8,128)S(1)} %get-tuple-element.43), channel_id=1, source_target_pairs={{1,0},{2,1},{3,2},{4,3},{5,4},{6,5},{7,6},{9,8},{10,9},{11,10},{12... | collective-permute-start | bytes 208904 | tf_op jit(solution)/shard_map/ppermute | solution.py:17
  60.4 7.9 %collective-permute-start.11 = (f32[2,34,1,256]{3,1,2,0:T(8,128)S(1)}, f32[2,34,1,256]{3,1,2,0:T(8,128)S(1)}, u32[]{:S(2)}, u32[]{:S(2)}) collective-permute-start(f32[2,34,1,256]{3,1,2,0:T(8,128)S(1)} %get-tuple-element.44), channel_id=1, source_target_pairs={{0,1},{1,2},{2,3},{3,4},{4,5},{5,6},{6,7},{8,9},{9,10},{10,11},{11... | collective-permute-start | bytes 208904 | tf_op jit(solution)/shard_map/ppermute | solution.py:16
  78.7 6.1 %collective-permute-start.14 = (f32[2,34,1,256]{3,1,2,0:T(8,128)S(1)}, f32[2,34,1,256]{3,1,2,0:T(8,128)S(1)}, u32[]{:S(2)}, u32[]{:S(2)}) collective-permute-start(f32[2,34,1,256]{3,1,2,0:T(8,128)S(1)} %get-tuple-element.41), channel_id=1, source_target_pairs={{1,0},{2,1},{3,2},{4,3},{5,4},{6,5},{7,6},{9,8},{10,9},{11,10},{12... | collective-permute-start | bytes 208904 | tf_op jit(solution)/shard_map/ppermute | solution.py:17
  89.6 8.2 %collective-permute-start.20 = (f32[2,1,32,256]{3,1,2,0:T(1,128)S(1)}, f32[2,1,32,256]{3,1,2,0:T(1,128)S(1)}, u32[]{:S(2)}, u32[]{:S(2)}) collective-permute-start(f32[2,1,32,256]{3,1,2,0:T(1,128)S(1)} %get-tuple-element.63), channel_id=1, source_target_pairs={{0,8},{8,16},{16,24},{1,9},{9,17},{17,25},{2,10},{10,18},{18,26},{... | collective-permute-start | bytes 196616 | tf_op jit(solution)/shard_map/ppermute | solution.py:16
  98.3 7.2 %collective-permute-start.22 = (f32[2,34,1,256]{3,1,2,0:T(8,128)S(1)}, f32[2,34,1,256]{3,1,2,0:T(8,128)S(1)}, u32[]{:S(2)}, u32[]{:S(2)}) collective-permute-start(f32[2,34,1,256]{3,1,2,0:T(8,128)S(1)} %get-tuple-element.39), channel_id=1, source_target_pairs={{0,1},{1,2},{2,3},{3,4},{4,5},{5,6},{6,7},{8,9},{9,10},{10,11},{11... | collective-permute-start | bytes 208904 | tf_op jit(solution)/shard_map/ppermute | solution.py:16
  102.6 6.4 %collective-permute-start.23 = (f32[2,34,1,256]{3,1,2,0:T(8,128)S(1)}, f32[2,34,1,256]{3,1,2,0:T(8,128)S(1)}, u32[]{:S(2)}, u32[]{:S(2)}) collective-permute-start(f32[2,34,1,256]{3,1,2,0:T(8,128)S(1)} %get-tuple-element.40), channel_id=1, source_target_pairs={{1,0},{2,1},{3,2},{4,3},{5,4},{6,5},{7,6},{9,8},{10,9},{11,10},{12... | collective-permute-start | bytes 208904 | tf_op jit(solution)/shard_map/ppermute | solution.py:17
  122.1 7.6 %collective-permute-start.26 = (f32[2,34,1,256]{3,1,2,0:T(8,128)S(1)}, f32[2,34,1,256]{3,1,2,0:T(8,128)S(1)}, u32[]{:S(2)}, u32[]{:S(2)}) collective-permute-start(f32[2,34,1,256]{3,1,2,0:T(8,128)S(1)} %get-tuple-element.37), channel_id=1, source_target_pairs={{0,1},{1,2},{2,3},{3,4},{4,5},{5,6},{6,7},{8,9},{9,10},{10,11},{11... | collective-permute-start | bytes 208904 | tf_op jit(solution)/shard_map/ppermute | solution.py:16
  185.8 6.2 %collective-permute-start.39 = (f32[2,34,1,256]{3,1,2,0:T(8,128)S(1)}, f32[2,34,1,256]{3,1,2,0:T(8,128)S(1)}, u32[]{:S(2)}, u32[]{:S(2)}) collective-permute-start(f32[2,34,1,256]{3,1,2,0:T(8,128)S(1)} %get-tuple-element.32), channel_id=1, source_target_pairs={{0,1},{1,2},{2,3},{3,4},{4,5},{5,6},{6,7},{8,9},{9,10},{10,11},{11... | collective-permute-start | bytes 208904 | tf_op jit(solution)/shard_map/ppermute | solution.py:16
  203.5 7.0 %collective-permute-start.43 = (f32[2,34,1,256]{3,1,2,0:T(8,128)S(1)}, f32[2,34,1,256]{3,1,2,0:T(8,128)S(1)}, u32[]{:S(2)}, u32[]{:S(2)}) collective-permute-start(f32[2,34,1,256]{3,1,2,0:T(8,128)S(1)} %get-tuple-element.30), channel_id=1, source_target_pairs={{0,1},{1,2},{2,3},{3,4},{4,5},{5,6},{6,7},{8,9},{9,10},{10,11},{11... | collective-permute-start | bytes 208904 | tf_op jit(solution)/shard_map/ppermute | solution.py:16
  239.1 7.5 %collective-permute-start.50 = (f32[2,34,1,256]{3,1,2,0:T(8,128)S(1)}, f32[2,34,1,256]{3,1,2,0:T(8,128)S(1)}, u32[]{:S(2)}, u32[]{:S(2)}) collective-permute-start(f32[2,34,1,256]{3,1,2,0:T(8,128)S(1)} %get-tuple-element.25), channel_id=1, source_target_pairs={{1,0},{2,1},{3,2},{4,3},{5,4},{6,5},{7,6},{9,8},{10,9},{11,10},{12... | collective-permute-start | bytes 208904 | tf_op jit(solution)/shard_map/ppermute | solution.py:17
  240.4 6.7 %collective-permute-start.51 = (f32[2,34,1,256]{3,1,2,0:T(8,128)S(1)}, f32[2,34,1,256]{3,1,2,0:T(8,128)S(1)}, u32[]{:S(2)}, u32[]{:S(2)}) collective-permute-start(f32[2,34,1,256]{3,1,2,0:T(8,128)S(1)} %get-tuple-element.26), channel_id=1, source_target_pairs={{0,1},{1,2},{2,3},{3,4},{4,5},{5,6},{6,7},{8,9},{9,10},{10,11},{11... | collective-permute-start | bytes 208904 | tf_op jit(solution)/shard_map/ppermute | solution.py:16
  439.6 30.3 %all-to-all-start.1 = ((f32[8,8,32,256]{3,2,1,0:T(8,128)}), f32[8,8,32,256]{3,2,1,0:T(8,128)S(1)}, u32[]{:S(2)}, u32[]{:S(2)}) async-start(f32[8,8,32,256]{3,2,1,0:T(8,128)} %copy.62), calls=%async_computation.1 | async-start | bytes 4194304 | tf_op jit(solution)/shard_map/all_to_all | solution.py:105
  (34 other events, 200.8 us)
where the time goes:
time: 481 us; the launch traced here: 472 us
  blocking collectives  152 us (32%)
  starting transfers between devices  147 us (31%)
  waiting for transfers between devices  66.8 us (14%)
  other arithmetic  53 us (11%)
  local copies, waits for them, and re-layouts  31.4 us (7%)
  matrix products  18.7 us (4%)
    ppermute x26, starting transfers between devices, extended(): before = lax.ppermute(last, axis, up)  109 us
    all_to_all x1, blocking collectives, shards(): lax.all_to_all(both, 'probe', split_axis=2, concat_axis=0, tiled=True)  79.6 us
    psum x1, blocking collectives, shards(): lax.psum(jnp.stack([partial_gram, partial_cross]), ('probe', 'sx', 'sy'))  72.6 us
    ppermute x26, starting transfers between devices, extended(): after = lax.ppermute(leading, axis, down)  34.3 us
    all_to_all x1, waiting for transfers between devices, shards(): lax.all_to_all(basis_slab.reshape(slabs[:, 0].shape), 'probe', split_axis...  25.3 us
    ppermute x26, waiting for transfers between devices, extended(): after = lax.ppermute(leading, axis, down)  24.1 us
    add x6, other arithmetic, forward_step(): result + (spread - 0.5 * cc[3]) * padded[..., 2:]  20.5 us
    ppermute x26, waiting for transfers between devices, extended(): before = lax.ppermute(last, axis, up)  17.3 us
  transfers between devices with their start and end apart: 53, of which 21 were waited for; matrix products, arithmetic and copies ran while one was open for 5% of the time, Pallas kernels for 0%

commit v1 on v0

--- a/solution.py
+++ b/solution.py
@@ -1,9 +1,18 @@
+import functools
 import jax
 import jax.numpy as jnp
 from jax import lax
 from jax.sharding import PartitionSpec as P
 
 STEPS = 4
+
+
+def check_set(tile_in, dev_axis, along_axis):
+    value_now = lax.psum(tile_in, axis_name=dev_axis)
+    return lax.psum(value_now, axis_name=along_axis)
+
+
+part_sources_all_here = functools.partial(check_set, dev_axis="probe", along_axis=("sx", "sy"))
 
 
 def extended(value, sides, width):
@@ -98,7 +107,7 @@
     flat_root = slabs[:, 1].reshape(count, -1)
     partial_gram = jnp.dot(flat, flat.T, precision=highest)
     partial_cross = jnp.dot(flat_root, flat_root.T, precision=highest)
-    sums = lax.psum(jnp.stack([partial_gram, partial_cross]), ("probe", "sx", "sy")) / ncells
+    sums = part_sources_all_here(jnp.stack([partial_gram, partial_cross])) / ncells
     gram, cross = (sums[0], sums[1])
     inverse = factor_inverse(gram, count)
     basis_slab = jnp.dot(inverse, flat, precision=highest)

time: 481 us -> 507 us (1.054)
  starting transfers between devices: 147 us -> 163 us
  blocking collectives: 152 us -> 163 us
    all_to_all x1, starting transfers between devices: 4.14 us -> 19.3 us  [shards(): lax.all_to_all(basis_slab.reshape(slabs[:, 0].shape), 'probe', split_axis...]
    psum x1 -> x2, blocking collectives: 72.6 us -> 83.7 us  [the longest x1 76 us: check_set(): return lax.psum(value_now, axis_name=along_axis)]
where the time goes in v1:
time: 507 us; the launch traced here: 498 us
  starting transfers between devices  163 us (32%)
  blocking collectives  163 us (32%)
  waiting for transfers between devices  66.8 us (13%)
  other arithmetic  53 us (10%)
  local copies, waits for them, and re-layouts  31.4 us (6%)
  matrix products  18.7 us (4%)
    ppermute x26, starting transfers between devices, extended(): before = lax.ppermute(last, axis, up)  109 us
    all_to_all x1, blocking collectives, shards(): lax.all_to_all(both, 'probe', split_axis=2, concat_axis=0, tiled=True)  79.6 us
    psum x1, blocking collectives, check_set(): return lax.psum(value_now, axis_name=along_axis)  76 us
    ppermute x26, starting transfers between devices, extended(): after = lax.ppermute(leading, axis, down)  34.3 us
    all_to_all x1, waiting for transfers between devices, shards(): lax.all_to_all(basis_slab.reshape(slabs[:, 0].shape), 'probe', split_axis...  25.3 us
    ppermute x26, waiting for transfers between devices, extended(): after = lax.ppermute(leading, axis, down)  24.1 us
    add x6, other arithmetic, forward_step(): result + (spread - 0.5 * cc[3]) * padded[..., 2:]  20.5 us
    all_to_all x1, starting transfers between devices, shards(): lax.all_to_all(basis_slab.reshape(slabs[:, 0].shape), 'probe', split_axis...  19.3 us
  transfers between devices with their start and end apart: 53, of which 21 were waited for; matrix products, arithmetic and copies ran while one was open for 5% of the time, Pallas kernels for 0%

profile of v1, /device:TPU:1, one launch (start us, length us, event | category | flops | bytes accessed | tf_op | source)
XLA Modules:
  0.0 497.9 jit_solution(16279369613025425369)
XLA Ops:
  3.0 4.6 collective-permute-start.1
  12.0 4.4 collective-permute-start.3
  33.3 4.9 collective-permute-start.7
  48.4 4.6 collective-permute-start.9
  53.3 4.4 collective-permute-start.18
  60.4 4.8 collective-permute-start.11
  73.1 4.3 collective-permute-start.13
  80.0 4.4 collective-permute-start.15
  98.3 4.3 collective-permute-start.22
  165.1 4.3 collective-permute-start.34
  203.5 4.4 collective-permute-start.43
  215.3 4.4 collective-permute-start.45
  222.4 4.4 collective-permute-start.47
  233.2 4.6 collective-permute-start.49
  240.4 5.3 %collective-permute-start.51 = (f32[2,34,1,256]{3,1,2,0:T(8,128)S(1)}, f32[2,34,1,256]{3,1,2,0:T(8,128)S(1)}, u32[]{:S(2)}, u32[]{:S(2)}) collective-permute-start(f32[2,34,1,256]{3,1,2,0:T(8,128)S(1)} %get-tuple-element.26), channel_id=1, source_target_pairs={{0,1},{1,2},{2,3},{3,4},{4,5},{5,6},{6,7},{8,9},{9,10},{10,11},{11... | collective-permute-start | bytes 208904 | tf_op jit(solution)/shard_map/ppermute | solution.py:25
  253.3 79.6 %all_to_all.36 = f32[2,2,32,32,256]{4,3,0,1,2:T(8,128)S(1)} all-to-all(f32[2,2,32,32,256]{4,3,0,1,2:T(8,128)S(1)} %copy.58), channel_id=1, replica_groups=mesh['probe'=4,'sx'=4,'sy'=8] {'probe'}, dimensions={2} | all-to-all | bytes 8388608 | tf_op jit(solution)/shard_map/all_to_all | solution.py:105
  333.0 5.2 %copy.72 = f32[2,2,4,8,32,256]{5,0,2,4,3,1:T(2,128)} copy(f32[2,2,4,8,32,256]{5,4,0,1,3,2:T(8,128)S(1)} %bitcast.90) | data formatting | bytes 8388608 | tf_op jit(solution)/shard_map/all_to_all | solution.py:105
  338.2 6.1 %all_to_all.29 = f32[8,2,8,32,256]{4,0,3,2,1:T(8,128)} reshape(f32[4,2,2,8,32,256]{5,1,0,4,3,2:T(2,128)} %bitcast.91) | data formatting | bytes 8388608 | tf_op jit(solution)/shard_map/all_to_all | solution.py:105
  344.4 7.1 %fusion.131 = f32[1,8,8]{2,1,0:T(8,128)S(1)} fusion(f32[8,2,8,32,256]{4,0,3,2,1:T(8,128)} %all_to_all.29), kind=kOutput, calls=%fused_computation.253 | convolution fusion | flops 50331648 | bytes 2097408 | tf_op jit(solution)/shard_map/dot_general | solution.py:108
  351.5 7.1 %fusion.134 = f32[1,8,8]{2,1,0:T(8,128)S(1)} fusion(f32[8,2,8,32,256]{4,0,3,2,1:T(8,128)} %all_to_all.29), kind=kOutput, calls=%fused_computation.254 | convolution fusion | flops 50331648 | bytes 2097408 | tf_op jit(solution)/shard_map/dot_general | solution.py:109
  358.6 7.6 %psum.14 = f32[2,8,8]{2,1,0:T(8,128)S(1)} all-reduce(f32[2,8,8]{2,1,0:T(8,128)S(1)} %pad_maximum_fusion.117), channel_id=1, replica_groups=mesh['probe'=4,'sx'=4,'sy'=8] {'probe'}, use_global_device_ids=true, to_apply=%region_0.1 | all-reduce | flops 128 | bytes 1024 | tf_op jit(solution)/shard_map/psum | solution.py:11
  366.2 76.0 %psum.15 = f32[2,8,8]{2,1,0:T(8,128)S(1)} all-reduce(f32[2,8,8]{2,1,0:T(8,128)S(1)} %psum.14), channel_id=1, replica_groups=mesh['probe'=4,'sx'=4,'sy'=8] {'sx','sy'}, use_global_device_ids=true, to_apply=%region_1.2 | all-reduce | flops 128 | bytes 1024 | tf_op jit(solution)/shard_map/psum | solution.py:12
  450.6 19.3 %all-to-all-start.1 = ((f32[8,8,32,256]{3,2,1,0:T(8,128)}), f32[8,8,32,256]{3,2,1,0:T(8,128)S(1)}, u32[]{:S(2)}, u32[]{:S(2)}) async-start(f32[8,8,32,256]{3,2,1,0:T(8,128)} %copy.62), calls=%async_computation.1 | async-start | bytes 4194304 | tf_op jit(solution)/shard_map/all_to_all | solution.py:114
  470.8 25.3 %all-to-all-done.1 = f32[8,8,32,256]{3,2,1,0:T(8,128)S(1)} async-done(((f32[8,8,32,256]{3,2,1,0:T(8,128)}), f32[8,8,32,256]{3,2,1,0:T(8,128)S(1)}, u32[]{:S(2)}, u32[]{:S(2)}) %all-to-all-start.1) | async-done | bytes 2097184 | tf_op jit(solution)/shard_map/all_to_all | solution.py:114
  (192 shorter events, 194.0 us)
Async XLA Ops:
  1.6 8.9 %collective-permute-start = (f32[2,1,32,256]{3,1,2,0:T(1,128)S(1)}, f32[2,1,32,256]{3,1,2,0:T(1,128)S(1)}, u32[]{:S(2)}, u32[]{:S(2)}) collective-permute-start(f32[2,1,32,256]{3,1,2,0:T(1,128)S(1)} %copy.38), channel_id=1, source_target_pairs={{8,0},{16,8},{24,16},{9,1},{17,9},{25,17},{10,2},{18,10},{26,18},{... | collective-permute-start | bytes 196616 | tf_op jit(solution)/shard_map/ppermute | solution.py:26
  3.0 7.6 %collective-permute-start.1 = (f32[2,1,32,256]{3,1,2,0:T(1,128)S(1)}, f32[2,1,32,256]{3,1,2,0:T(1,128)S(1)}, u32[]{:S(2)}, u32[]{:S(2)}) collective-permute-start(f32[2,1,32,256]{3,1,2,0:T(1,128)S(1)} %copy.41), channel_id=1, source_target_pairs={{0,8},{8,16},{16,24},{1,9},{9,17},{17,25},{2,10},{10,18},{18,26},{... | collective-permute-start | bytes 196616 | tf_op jit(solution)/shard_map/ppermute | solution.py:25
  10.6 11.2 %collective-permute-start.2 = (f32[2,34,1,256]{3,1,2,0:T(8,128)S(1)}, f32[2,34,1,256]{3,1,2,0:T(8,128)S(1)}, u32[]{:S(2)}, u32[]{:S(2)}) collective-permute-start(f32[2,34,1,256]{3,1,2,0:T(8,128)S(1)} %get-tuple-element.47), channel_id=1, source_target_pairs={{1,0},{2,1},{3,2},{4,3},{5,4},{6,5},{7,6},{9,8},{10,9},{11,10},{12... | collective-permute-start | bytes 208904 | tf_op jit(solution)/shard_map/ppermute | solution.py:26
  12.0 9.8 %collective-permute-start.3 = (f32[2,34,1,256]{3,1,2,0:T(8,128)S(1)}, f32[2,34,1,256]{3,1,2,0:T(8,128)S(1)}, u32[]{:S(2)}, u32[]{:S(2)}) collective-permute-start(f32[2,34,1,256]{3,1,2,0:T(8,128)S(1)} %get-tuple-element.48), channel_id=1, source_target_pairs={{0,1},{1,2},{2,3},{3,4},{4,5},{5,6},{6,7},{8,9},{9,10},{10,11},{11... | collective-permute-start | bytes 208904 | tf_op jit(solution)/shard_map/ppermute | solution.py:25
  32.0 11.5 %collective-permute-start.6 = (f32[2,34,1,256]{3,1,2,0:T(8,128)S(1)}, f32[2,34,1,256]{3,1,2,0:T(8,128)S(1)}, u32[]{:S(2)}, u32[]{:S(2)}) collective-permute-start(f32[2,34,1,256]{3,1,2,0:T(8,128)S(1)} %get-tuple-element.45), channel_id=1, source_target_pairs={{1,0},{2,1},{3,2},{4,3},{5,4},{6,5},{7,6},{9,8},{10,9},{11,10},{12... | collective-permute-start | bytes 208904 | tf_op jit(solution)/shard_map/ppermute | solution.py:26
  33.3 10.2 %collective-permute-start.7 = (f32[2,34,1,256]{3,1,2,0:T(8,128)S(1)}, f32[2,34,1,256]{3,1,2,0:T(8,128)S(1)}, u32[]{:S(2)}, u32[]{:S(2)}) collective-permute-start(f32[2,34,1,256]{3,1,2,0:T(8,128)S(1)} %get-tuple-element.46), channel_id=1, source_target_pairs={{0,1},{1,2},{2,3},{3,4},{4,5},{5,6},{6,7},{8,9},{9,10},{10,11},{11... | collective-permute-start | bytes 208904 | tf_op jit(solution)/shard_map/ppermute | solution.py:25
  38.3 14.8 %collective-permute-start.16 = (f32[4,1,32,256]{3,2,1,0:T(8,128)S(1)}, f32[4,1,32,256]{3,2,1,0:T(8,128)S(1)}, u32[]{:S(2)}, u32[]{:S(2)}) collective-permute-start(f32[4,1,32,256]{3,2,1,0:T(8,128)S(1)} %get-tuple-element.17), channel_id=1, source_target_pairs={{0,8},{8,16},{16,24},{1,9},{9,17},{17,25},{2,10},{10,18},{18,26},{... | collective-permute-start | bytes 393224 | tf_op jit(solution)/shard_map/ppermute | solution.py:25
  42.3 10.8 %collective-permute-start.17 = (f32[4,1,32,256]{3,2,1,0:T(8,128)S(1)}, f32[4,1,32,256]{3,2,1,0:T(8,128)S(1)}, u32[]{:S(2)}, u32[]{:S(2)}) collective-permute-start(f32[4,1,32,256]{3,2,1,0:T(8,128)S(1)} %get-tuple-element.18), channel_id=1, source_target_pairs={{8,0},{16,8},{24,16},{9,1},{17,9},{25,17},{10,2},{18,10},{26,18},{... | collective-permute-start | bytes 393224 | tf_op jit(solution)/shard_map/ppermute | solution.py:26
  47.1 11.9 %collective-permute-start.8 = (f32[2,1,32,256]{3,1,2,0:T(1,128)S(1)}, f32[2,1,32,256]{3,1,2,0:T(1,128)S(1)}, u32[]{:S(2)}, u32[]{:S(2)}) collective-permute-start(f32[2,1,32,256]{3,1,2,0:T(1,128)S(1)} %get-tuple-element.68), channel_id=1, source_target_pairs={{8,0},{16,8},{24,16},{9,1},{17,9},{25,17},{10,2},{18,10},{26,18},{... | collective-permute-start | bytes 196616 | tf_op jit(solution)/shard_map/ppermute | solution.py:26
  48.4 10.6 %collective-permute-start.9 = (f32[2,1,32,256]{3,1,2,0:T(1,128)S(1)}, f32[2,1,32,256]{3,1,2,0:T(1,128)S(1)}, u32[]{:S(2)}, u32[]{:S(2)}) collective-permute-start(f32[2,1,32,256]{3,1,2,0:T(1,128)S(1)} %get-tuple-element.67), channel_id=1, source_target_pairs={{0,8},{8,16},{16,24},{1,9},{9,17},{17,25},{2,10},{10,18},{18,26},{... | collective-permute-start | bytes 196616 | tf_op jit(solution)/shard_map/ppermute | solution.py:25
  53.3 12.5 %collective-permute-start.18 = (f32[4,34,1,256]{3,1,2,0:T(8,128)S(1)}, f32[4,34,1,256]{3,1,2,0:T(8,128)S(1)}, u32[]{:S(2)}, u32[]{:S(2)}) collective-permute-start(f32[4,34,1,256]{3,1,2,0:T(8,128)S(1)} %copy.49), channel_id=1, source_target_pairs={{0,1},{1,2},{2,3},{3,4},{4,5},{5,6},{6,7},{8,9},{9,10},{10,11},{11... | collective-permute-start | bytes 417800 | tf_op jit(solution)/shard_map/ppermute | solution.py:25
  57.8 8.2 %collective-permute-start.19 = (f32[4,34,1,256]{3,1,2,0:T(8,128)S(1)}, f32[4,34,1,256]{3,1,2,0:T(8,128)S(1)}, u32[]{:S(2)}, u32[]{:S(2)}) collective-permute-start(f32[4,34,1,256]{3,1,2,0:T(8,128)S(1)} %copy.50), channel_id=1, source_target_pairs={{1,0},{2,1},{3,2},{4,3},{5,4},{6,5},{7,6},{9,8},{10,9},{11,10},{12... | collective-permute-start | bytes 417800 | tf_op jit(solution)/shard_map/ppermute | solution.py:26
  59.1 7.1 %collective-permute-start.10 = (f32[2,34,1,256]{3,1,2,0:T(8,128)S(1)}, f32[2,34,1,256]{3,1,2,0:T(8,128)S(1)}, u32[]{:S(2)}, u32[]{:S(2)}) collective-permute-start(f32[2,34,1,256]{3,1,2,0:T(8,128)S(1)} %get-tuple-element.43), channel_id=1, source_target_pairs={{1,0},{2,1},{3,2},{4,3},{5,4},{6,5},{7,6},{9,8},{10,9},{11,10},{12... | collective-permute-start | bytes 208904 | tf_op jit(solution)/shard_map/ppermute | solution.py:26
  60.4 7.9 %collective-permute-start.11 = (f32[2,34,1,256]{3,1,2,0:T(8,128)S(1)}, f32[2,34,1,256]{3,1,2,0:T(8,128)S(1)}, u32[]{:S(2)}, u32[]{:S(2)}) collective-permute-start(f32[2,34,1,256]{3,1,2,0:T(8,128)S(1)} %get-tuple-element.44), channel_id=1, source_target_pairs={{0,1},{1,2},{2,3},{3,4},{4,5},{5,6},{6,7},{8,9},{9,10},{10,11},{11... | collective-permute-start | bytes 208904 | tf_op jit(solution)/shard_map/ppermute | solution.py:25
  78.7 6.1 %collective-permute-start.14 = (f32[2,34,1,256]{3,1,2,0:T(8,128)S(1)}, f32[2,34,1,256]{3,1,2,0:T(8,128)S(1)}, u32[]{:S(2)}, u32[]{:S(2)}) collective-permute-start(f32[2,34,1,256]{3,1,2,0:T(8,128)S(1)} %get-tuple-element.41), channel_id=1, source_target_pairs={{1,0},{2,1},{3,2},{4,3},{5,4},{6,5},{7,6},{9,8},{10,9},{11,10},{12... | collective-permute-start | bytes 208904 | tf_op jit(solution)/shard_map/ppermute | solution.py:26
  89.6 8.2 %collective-permute-start.20 = (f32[2,1,32,256]{3,1,2,0:T(1,128)S(1)}, f32[2,1,32,256]{3,1,2,0:T(1,128)S(1)}, u32[]{:S(2)}, u32[]{:S(2)}) collective-permute-start(f32[2,1,32,256]{3,1,2,0:T(1,128)S(1)} %get-tuple-element.63), channel_id=1, source_target_pairs={{0,8},{8,16},{16,24},{1,9},{9,17},{17,25},{2,10},{10,18},{18,26},{... | collective-permute-start | bytes 196616 | tf_op jit(solution)/shard_map/ppermute | solution.py:25
  98.3 7.2 %collective-permute-start.22 = (f32[2,34,1,256]{3,1,2,0:T(8,128)S(1)}, f32[2,34,1,256]{3,1,2,0:T(8,128)S(1)}, u32[]{:S(2)}, u32[]{:S(2)}) collective-permute-start(f32[2,34,1,256]{3,1,2,0:T(8,128)S(1)} %get-tuple-element.39), channel_id=1, source_target_pairs={{0,1},{1,2},{2,3},{3,4},{4,5},{5,6},{6,7},{8,9},{9,10},{10,11},{11... | collective-permute-start | bytes 208904 | tf_op jit(solution)/shard_map/ppermute | solution.py:25
  102.6 6.4 %collective-permute-start.23 = (f32[2,34,1,256]{3,1,2,0:T(8,128)S(1)}, f32[2,34,1,256]{3,1,2,0:T(8,128)S(1)}, u32[]{:S(2)}, u32[]{:S(2)}) collective-permute-start(f32[2,34,1,256]{3,1,2,0:T(8,128)S(1)} %get-tuple-element.40), channel_id=1, source_target_pairs={{1,0},{2,1},{3,2},{4,3},{5,4},{6,5},{7,6},{9,8},{10,9},{11,10},{12... | collective-permute-start | bytes 208904 | tf_op jit(solution)/shard_map/ppermute | solution.py:26
  122.1 7.6 %collective-permute-start.26 = (f32[2,34,1,256]{3,1,2,0:T(8,128)S(1)}, f32[2,34,1,256]{3,1,2,0:T(8,128)S(1)}, u32[]{:S(2)}, u32[]{:S(2)}) collective-permute-start(f32[2,34,1,256]{3,1,2,0:T(8,128)S(1)} %get-tuple-element.37), channel_id=1, source_target_pairs={{0,1},{1,2},{2,3},{3,4},{4,5},{5,6},{6,7},{8,9},{9,10},{10,11},{11... | collective-permute-start | bytes 208904 | tf_op jit(solution)/shard_map/ppermute | solution.py:25
  185.8 6.2 %collective-permute-start.39 = (f32[2,34,1,256]{3,1,2,0:T(8,128)S(1)}, f32[2,34,1,256]{3,1,2,0:T(8,128)S(1)}, u32[]{:S(2)}, u32[]{:S(2)}) collective-permute-start(f32[2,34,1,256]{3,1,2,0:T(8,128)S(1)} %get-tuple-element.32), channel_id=1, source_target_pairs={{0,1},{1,2},{2,3},{3,4},{4,5},{5,6},{6,7},{8,9},{9,10},{10,11},{11... | collective-permute-start | bytes 208904 | tf_op jit(solution)/shard_map/ppermute | solution.py:25
  203.5 7.0 %collective-permute-start.43 = (f32[2,34,1,256]{3,1,2,0:T(8,128)S(1)}, f32[2,34,1,256]{3,1,2,0:T(8,128)S(1)}, u32[]{:S(2)}, u32[]{:S(2)}) collective-permute-start(f32[2,34,1,256]{3,1,2,0:T(8,128)S(1)} %get-tuple-element.30), channel_id=1, source_target_pairs={{0,1},{1,2},{2,3},{3,4},{4,5},{5,6},{6,7},{8,9},{9,10},{10,11},{11... | collective-permute-start | bytes 208904 | tf_op jit(solution)/shard_map/ppermute | solution.py:25
  239.1 7.5 %collective-permute-start.50 = (f32[2,34,1,256]{3,1,2,0:T(8,128)S(1)}, f32[2,34,1,256]{3,1,2,0:T(8,128)S(1)}, u32[]{:S(2)}, u32[]{:S(2)}) collective-permute-start(f32[2,34,1,256]{3,1,2,0:T(8,128)S(1)} %get-tuple-element.25), channel_id=1, source_target_pairs={{1,0},{2,1},{3,2},{4,3},{5,4},{6,5},{7,6},{9,8},{10,9},{11,10},{12... | collective-permute-start | bytes 208904 | tf_op jit(solution)/shard_map/ppermute | solution.py:26
  240.4 6.7 %collective-permute-start.51 = (f32[2,34,1,256]{3,1,2,0:T(8,128)S(1)}, f32[2,34,1,256]{3,1,2,0:T(8,128)S(1)}, u32[]{:S(2)}, u32[]{:S(2)}) collective-permute-start(f32[2,34,1,256]{3,1,2,0:T(8,128)S(1)} %get-tuple-element.26), channel_id=1, source_target_pairs={{0,1},{1,2},{2,3},{3,4},{4,5},{5,6},{6,7},{8,9},{9,10},{10,11},{11... | collective-permute-start | bytes 208904 | tf_op jit(solution)/shard_map/ppermute | solution.py:25
  450.6 45.5 %all-to-all-start.1 = ((f32[8,8,32,256]{3,2,1,0:T(8,128)}), f32[8,8,32,256]{3,2,1,0:T(8,128)S(1)}, u32[]{:S(2)}, u32[]{:S(2)}) async-start(f32[8,8,32,256]{3,2,1,0:T(8,128)} %copy.62), calls=%async_computation.1 | async-start | bytes 4194304 | tf_op jit(solution)/shard_map/all_to_all | solution.py:114
  (34 other events, 200.8 us)
